TPU v7x, 32 devices: a whole 2x2x4 slice. The times are simulated.
32 devices in a mesh: shard: 4 (over z), ctx: 2 (over y), tp: 4 (over x, core).
Axes of the slice: x: 2, y: 2, z: 4, core: 2. Of those that a mesh axis runs over, the one named last changes fastest.
Arguments:
- inputs: float32 [8, 256, 1024], P('shard', 'ctx'), may hold values from -12 to 12
- segment_ids: int32 [8, 256], P('shard', 'ctx'), may hold values from 0 to 3, never falling along the last dimension, each value on 1 to 128 neighbouring positions
- gains: bfloat16 [2, 1024], P(None, ('shard', 'ctx')), may hold values from 0.5 to 1.5
- shifts: bfloat16 [2, 1024], P(None, ('shard', 'ctx')), may hold values from -3 to 3
- attend_weight: bfloat16 [1024, 3, 1024], P(('shard', 'ctx'), None, 'tp'), may hold values from -1 to 1
- merge_weight: bfloat16 [1024, 1024], P(('shard', 'ctx'), 'tp'), may hold values from -0.75 to 0.75
- expand_weight: bfloat16 [1024, 4096], P(('shard', 'ctx'), 'tp'), may hold values from -0.1875 to 0.1875
- expand_bias: bfloat16 [4, 1024], P('tp', ('shard', 'ctx')), may hold values from -3 to 3
- reduce_weight: bfloat16 [1024, 4096], P(('shard', 'ctx'), 'tp'), may hold values from -0.09375 to 0.09375
- cotangent: float32 [8, 256, 1024], P('shard', 'ctx'), may hold values from -6 to 6
Outputs:
- block_out: float32 [8, 256, 1024], P('shard', 'ctx')
- input_grad: float32 [8, 256, 1024], P('shard', 'ctx')
- gains_grad: float32 [2, 1024], P(None, ('shard', 'ctx'))
- shifts_grad: float32 [2, 1024], P(None, ('shard', 'ctx'))
- attend_grad: float32 [1024, 3, 1024], P(('shard', 'ctx'), None, 'tp')
- merge_grad: float32 [1024, 1024], P(('shard', 'ctx'), 'tp')
- expand_grad: float32 [1024, 4096], P(('shard', 'ctx'), 'tp')
- bias_grad: float32 [4, 1024], P('tp', ('shard', 'ctx'))
- reduce_grad: float32 [1024, 4096], P(('shard', 'ctx'), 'tp')
Inputs may be any that keep to these rules, and one draw needn't show every extreme that they name: `segment_ids`: within each sequence segment ids never fall; every document holds 1 to 128 tokens, and one of them exactly 128.
All inputs are finite; a program needn't handle non-finite values.
Results may differ from a plain program's by a relative error of at most 0.0093.
Values may be sent and summed in bfloat16 or wider, within the bound.
No kernel may reach another device: no remote copies, remote signals or barrier semaphores. Data moves between devices by JAX's collectives and lax.ppermute only.
A program may use at most 128 MiB of HBM per device.

v0:
```python
import jax
import jax.numpy as jnp
from jax import lax
from jax.sharding import PartitionSpec as P

HD = 64
epsilon = 1e-05
masked_score = -1e30
gelu_scale = 0.7978845608028654
gelu_cubic = 0.044715


def norm_forward(values, gain, shift):
    average = jnp.mean(values, axis=-1, keepdims=True)
    centered = values - average
    variance = jnp.mean(centered * centered, axis=-1, keepdims=True)
    inverse = lax.rsqrt(variance + epsilon)
    normed = centered * inverse
    return (normed, inverse, normed * gain.astype(jnp.float32) + shift.astype(jnp.float32))


def norm_backward(upstream, normed, inverse, gain):
    scaled = upstream * gain.astype(jnp.float32)
    first_mean = jnp.mean(scaled, axis=-1, keepdims=True)
    second_mean = jnp.mean(scaled * normed, axis=-1, keepdims=True)
    return inverse * (scaled - first_mean - normed * second_mean)


def gelu_pair(pre_act):
    inner_arg = gelu_scale * (pre_act + gelu_cubic * pre_act * pre_act * pre_act)
    tangent = jnp.tanh(inner_arg)
    gelu_value = 0.5 * pre_act * (1.0 + tangent)
    gelu_slope = 0.5 * (1.0 + tangent) + 0.5 * pre_act * (1.0 - tangent * tangent) * gelu_scale * (
        1.0 + 3.0 * gelu_cubic * pre_act * pre_act
    )
    return (gelu_value, gelu_slope)


def shards(
    inputs,
    segment_ids,
    gains,
    shifts,
    attend_weight,
    merge_weight,
    expand_weight,
    expand_bias,
    reduce_weight,
    cotangent,
):
    seq_count, group_len, model_width = inputs.shape
    row_count = seq_count * group_len
    full_len = group_len * lax.axis_size("ctx")
    head_scale = HD ** (-0.5)
    gathered = (
        lax.all_gather(attend_weight, ("shard", "ctx"), axis=0, tiled=True),
        lax.all_gather(merge_weight, ("shard", "ctx"), axis=0, tiled=True),
        lax.all_gather(expand_weight, ("shard", "ctx"), axis=0, tiled=True),
        lax.all_gather(reduce_weight, ("shard", "ctx"), axis=0, tiled=True),
        lax.all_gather(expand_bias, ("shard", "ctx"), axis=1, tiled=True),
        lax.all_gather(gains, ("shard", "ctx"), axis=1, tiled=True),
        lax.all_gather(shifts, ("shard", "ctx"), axis=1, tiled=True),
    )
    attend_full, merge_full, expand_full, reduce_full, bias_full, gains_full, shifts_full = gathered
    local_cols = attend_full.shape[2]
    head_local = local_cols // HD
    flat_in = inputs.reshape(row_count, model_width)
    normed_early, inverse_early, affine_early = norm_forward(flat_in, gains_full[0], shifts_full[0])
    hidden_early = affine_early.astype(jnp.bfloat16)
    projected = jnp.einsum(
        "rd,dtc->rtc", hidden_early, attend_full, preferred_element_type=jnp.float32
    )
    query_heads = (
        (projected[:, 0] * head_scale)
        .astype(jnp.bfloat16)
        .reshape(seq_count, group_len, head_local, HD)
    )
    key_rows = projected[:, 1].astype(jnp.bfloat16).reshape(seq_count, group_len, local_cols)
    value_rows = projected[:, 2].astype(jnp.bfloat16).reshape(seq_count, group_len, local_cols)
    all_keys, all_values, all_segments = (
        lax.all_gather(key_rows, "ctx", axis=1, tiled=True),
        lax.all_gather(value_rows, "ctx", axis=1, tiled=True),
        lax.all_gather(segment_ids, "ctx", axis=1, tiled=True),
    )
    key_heads = all_keys.reshape(seq_count, full_len, head_local, HD)
    value_heads = all_values.reshape(seq_count, full_len, head_local, HD)
    query_pos = lax.axis_index("ctx") * group_len + jnp.arange(group_len, dtype=jnp.int32)
    key_pos = jnp.arange(full_len, dtype=jnp.int32)
    allowed = (segment_ids[:, :, None] == all_segments[:, None, :]) & (
        key_pos[None, None, :] <= query_pos[None, :, None]
    )
    allowed = allowed[:, None]

    def score_block():
        raw_scores = jnp.einsum(
            "sqhd,skhd->shqk", query_heads, key_heads, preferred_element_type=jnp.float32
        )
        return jnp.where(allowed, raw_scores, masked_score)

    scores = score_block()
    row_top = jnp.max(scores, axis=-1, keepdims=True)
    log_total = row_top + jnp.log(jnp.sum(jnp.exp(scores - row_top), axis=-1, keepdims=True))
    attn_probs = jnp.exp(scores - log_total)
    probs_half = attn_probs.astype(jnp.bfloat16)
    attended_heads = jnp.einsum(
        "shqk,skhd->sqhd", probs_half, value_heads, preferred_element_type=jnp.float32
    ).astype(jnp.bfloat16)
    attended = attended_heads.reshape(row_count, local_cols)
    merge_part = jnp.einsum("rc,oc->ro", attended, merge_full, preferred_element_type=jnp.float32)
    residual = flat_in + lax.psum(merge_part, "tp")
    normed_later, inverse_later, affine_later = norm_forward(
        residual, gains_full[1], shifts_full[1]
    )
    hidden_later = affine_later.astype(jnp.bfloat16)
    pre_act = jnp.dot(
        hidden_later, expand_full, preferred_element_type=jnp.float32
    ) + bias_full.astype(jnp.float32)
    gelu_value, gelu_slope = gelu_pair(pre_act)
    activated = gelu_value.astype(jnp.bfloat16)
    reduce_part = jnp.einsum(
        "rf,of->ro", activated, reduce_full, preferred_element_type=jnp.float32
    )
    block_out = residual + lax.psum(reduce_part.astype(jnp.bfloat16), "tp").astype(jnp.float32)
    back_set = (
        lax.all_gather(attend_weight, ("shard", "ctx"), axis=0, tiled=True),
        lax.all_gather(merge_weight, ("shard", "ctx"), axis=0, tiled=True),
        lax.all_gather(expand_weight, ("shard", "ctx"), axis=0, tiled=True),
        lax.all_gather(reduce_weight, ("shard", "ctx"), axis=0, tiled=True),
        lax.all_gather(gains, ("shard", "ctx"), axis=1, tiled=True),
    )
    attend_back, merge_back, expand_back, reduce_back, gains_back = back_set
    output_grad = cotangent.reshape(row_count, model_width)
    cot_half = output_grad.astype(jnp.bfloat16)
    reduce_grad = jnp.einsum("ro,rf->of", cot_half, activated, preferred_element_type=jnp.float32)
    pre_grad = jnp.dot(cot_half, reduce_back, preferred_element_type=jnp.float32) * gelu_slope
    pre_half = pre_grad.astype(jnp.bfloat16)
    bias_grad = jnp.sum(pre_grad, axis=0, keepdims=True)
    expand_grad = jnp.einsum(
        "rd,rf->df", hidden_later, pre_half, preferred_element_type=jnp.float32
    )
    later_part = jnp.einsum("rf,df->rd", pre_half, expand_back, preferred_element_type=jnp.float32)
    later_grad = lax.psum(later_part, "tp")
    residual_grad = output_grad + norm_backward(
        later_grad, normed_later, inverse_later, gains_back[1]
    )
    resid_half = residual_grad.astype(jnp.bfloat16)
    merge_grad = jnp.einsum("ro,rc->oc", resid_half, attended, preferred_element_type=jnp.float32)
    attended_grad = jnp.dot(resid_half, merge_back, preferred_element_type=jnp.float32).astype(
        jnp.bfloat16
    )
    grad_heads = attended_grad.reshape(seq_count, group_len, head_local, HD)
    scores_again = score_block()
    probs_again = jnp.exp(scores_again - log_total)
    probs_again_half = probs_again.astype(jnp.bfloat16)
    row_delta = jnp.einsum(
        "sqhd,sqhd->shq", grad_heads, attended_heads, preferred_element_type=jnp.float32
    )
    prob_grad = jnp.einsum(
        "sqhd,skhd->shqk", grad_heads, value_heads, preferred_element_type=jnp.float32
    )
    score_grad = probs_again * (prob_grad - row_delta[..., None])
    score_half = score_grad.astype(jnp.bfloat16)
    query_grad = (
        jnp.einsum("shqk,skhd->sqhd", score_half, key_heads, preferred_element_type=jnp.float32)
        * head_scale
    )
    keys_part = jnp.einsum(
        "shqk,sqhd->skhd", score_half, query_heads, preferred_element_type=jnp.float32
    ).reshape(seq_count, full_len, local_cols)
    values_part = jnp.einsum(
        "shqk,sqhd->skhd", probs_again_half, grad_heads, preferred_element_type=jnp.float32
    ).reshape(seq_count, full_len, local_cols)
    keys_grad, values_grad = (
        lax.psum_scatter(keys_part, "ctx", scatter_dimension=1, tiled=True),
        lax.psum_scatter(values_part, "ctx", scatter_dimension=1, tiled=True),
    )
    proj_grad = jnp.stack(
        [
            query_grad.reshape(row_count, local_cols),
            keys_grad.reshape(row_count, local_cols),
            values_grad.reshape(row_count, local_cols),
        ],
        axis=1,
    ).astype(jnp.bfloat16)
    attend_grad = jnp.einsum(
        "rd,rtc->dtc", hidden_early, proj_grad, preferred_element_type=jnp.float32
    )
    early_part = jnp.einsum(
        "rtc,dtc->rd", proj_grad, attend_back, preferred_element_type=jnp.float32
    )
    early_grad = lax.psum(early_part, "tp")
    input_grad = residual_grad + norm_backward(
        early_grad, normed_early, inverse_early, gains_back[0]
    )
    gains_grad = jnp.stack(
        [jnp.sum(early_grad * normed_early, axis=0), jnp.sum(later_grad * normed_later, axis=0)]
    )
    shifts_grad = jnp.stack([jnp.sum(early_grad, axis=0), jnp.sum(later_grad, axis=0)])
    shares = (
        lax.psum_scatter(attend_grad, ("shard", "ctx"), scatter_dimension=0, tiled=True),
        lax.psum_scatter(merge_grad, ("shard", "ctx"), scatter_dimension=0, tiled=True),
        lax.psum_scatter(expand_grad, ("shard", "ctx"), scatter_dimension=0, tiled=True),
        lax.psum_scatter(reduce_grad, ("shard", "ctx"), scatter_dimension=0, tiled=True),
        lax.psum_scatter(bias_grad, ("shard", "ctx"), scatter_dimension=1, tiled=True),
        lax.psum_scatter(gains_grad, ("shard", "ctx"), scatter_dimension=1, tiled=True),
        lax.psum_scatter(shifts_grad, ("shard", "ctx"), scatter_dimension=1, tiled=True),
    )
    return (
        block_out.reshape(inputs.shape),
        input_grad.reshape(inputs.shape),
        shares[5],
        shares[6],
        shares[0],
        shares[1],
        shares[2],
        shares[4],
        shares[3],
    )


def solution(mesh):
    in_specs = (
        P("shard", "ctx", None),
        P("shard", "ctx"),
        P(None, ("shard", "ctx")),
        P(None, ("shard", "ctx")),
        P(("shard", "ctx"), None, "tp"),
        P(("shard", "ctx"), "tp"),
        P(("shard", "ctx"), "tp"),
        P("tp", ("shard", "ctx")),
        P(("shard", "ctx"), "tp"),
        P("shard", "ctx", None),
    )
    out_specs = (
        P("shard", "ctx", None),
        P("shard", "ctx", None),
        P(None, ("shard", "ctx")),
        P(None, ("shard", "ctx")),
        P(("shard", "ctx"), None, "tp"),
        P(("shard", "ctx"), "tp"),
        P(("shard", "ctx"), "tp"),
        P("tp", ("shard", "ctx")),
        P(("shard", "ctx"), "tp"),
    )
    return jax.shard_map(shards, mesh=mesh, in_specs=in_specs, out_specs=out_specs, check_vma=False)
```

profile of v0, /device:TPU:0, one launch (start us, length us, event | category | flops | bytes accessed | tf_op | source)
XLA Modules:
  0.0 930.5 jit_solution(1876446625818564370)
XLA Ops:
  9.4 5.5 all_gather.39
  14.8 21.4 %all_gather.35 = bf16[2,1024]{1,0:T(2,128)(2,1)S(1)} all-gather(bf16[2,128]{1,0:T(2,128)(2,1)} %param.12), channel_id=1, replica_groups=mesh['shard'=4,'ctx'=2,'tp'=4] {'shard','ctx'}, dimensions={1}, use_global_device_ids=true | all-gather | bytes 4608 | tf_op jit(solution)/shard_map/all_gather | solution.py:61
  36.3 16.5 %all_gather.36 = bf16[2,1024]{1,0:T(2,128)(2,1)S(1)} all-gather(bf16[2,128]{1,0:T(2,128)(2,1)} %param.13), channel_id=1, replica_groups=mesh['shard'=4,'ctx'=2,'tp'=4] {'shard','ctx'}, dimensions={1}, use_global_device_ids=true | all-gather | bytes 4608 | tf_op jit(solution)/shard_map/all_gather | solution.py:62
  54.6 31.4 %all_gather.41 = bf16[1024,256]{1,0:T(8,128)(2,1)S(1)} all-gather(bf16[128,256]{1,0:T(8,128)(2,1)S(1)} %copy-done.16), channel_id=1, replica_groups=mesh['shard'=4,'ctx'=2,'tp'=4] {'shard','ctx'}, dimensions={0}, use_global_device_ids=true | all-gather | bytes 589824 | tf_op jit(solution)/shard_map/all_gather | solution.py:57
  88.5 5.6 all_gather.38
  95.0 5.6 all_gather.40
  105.7 18.4 %all_gather.43 = bf16[1,1024]{1,0:T(2,128)(2,1)S(1)} all-gather(bf16[1,128]{1,0:T(2,128)(2,1)S(1)} %copy-done.31), channel_id=1, replica_groups=mesh['shard'=4,'ctx'=2,'tp'=4] {'shard','ctx'}, dimensions={1}, use_global_device_ids=true | all-gather | bytes 2304 | tf_op jit(solution)/shard_map/all_gather | solution.py:60
  126.3 13.4 %all-reduce.5.cloned.1.call-done = f32[256,1024]{1,0:T(8,128)} async-done(((f32[256,1024]{1,0:T(8,128)}), f32[256,1024]{1,0:T(8,128)}) %all-reduce.5.cloned.1.call-update) | async-done | bytes 1048592 | tf_op jit(solution)/shard_map/psum | solution.py:110
  141.3 50.0 %all-gather.6.cloned.1.call-done = bf16[1024,1024]{1,0:T(8,128)(2,1)} async-done(((bf16[128,1024]{1,0:T(8,128)(2,1)}), bf16[1024,1024]{1,0:T(8,128)(2,1)}) %all-gather.6.cloned.1.call-update) | async-done | bytes 2097168 | tf_op jit(solution)/shard_map/all_gather | solution.py:58
  191.4 3.3 convolution_add_fusion
  194.7 46.3 %all-gather.8.cloned.1.call-done = bf16[1024,1024]{1,0:T(8,128)(2,1)} async-done(((bf16[128,1024]{1,0:T(8,128)(2,1)}), bf16[1024,1024]{1,0:T(8,128)(2,1)}) %all-gather.8.cloned.1.call-update) | async-done | bytes 2097168 | tf_op jit(solution)/shard_map/all_gather | solution.py:59
  241.0 3.9 fusion.40
  247.5 3.5 convolution_convert_fusion
  251.1 31.3 %all-reduce.9.cloned.1.call-done = f32[256,1024]{1,0:T(8,128)} async-done(((f32[256,1024]{1,0:T(8,128)}), f32[256,1024]{1,0:T(8,128)}) %all-reduce.9.cloned.1.call-update) | async-done | bytes 1048592 | tf_op jit(solution)/shard_map/psum | solution.py:142
  282.4 2.3 multiply_reduce_fusion
  284.8 34.3 %all-reduce.7.cloned.1.call-done = bf16[256,1024]{1,0:T(8,128)(2,1)} async-done(((bf16[256,1024]{1,0:T(8,128)(2,1)}), bf16[256,1024]{1,0:T(8,128)(2,1)}) %all-reduce.7.cloned.1.call-update) | async-done | bytes 524304 | tf_op jit(solution)/shard_map/psum | solution.py:123
  319.1 3.0 bitcast_add_fusion
  332.5 8.7 reduce-scatter.18.cloned.1.call-done
  342.3 15.8 %reduce-scatter.16.cloned.1.call-done = f32[2,128,256]{1,2,0:T(8,128)} async-done(((f32[2,256,256]{1,2,0:T(8,128)}), f32[2,128,256]{1,2,0:T(8,128)}) %reduce-scatter.16.cloned.1.call-update) | async-done | bytes 262160 | tf_op jit(solution)/shard_map/reduce_scatter | solution.py:174
  359.2 3.0 convolution_bitcast_fusion.1
  363.6 35.1 %all-reduce.11.cloned.1.call-done = f32[256,1024]{1,0:T(8,128)} async-done(((f32[256,1024]{1,0:T(8,128)}), f32[256,1024]{1,0:T(8,128)}) %all-reduce.11.cloned.1.call-update) | async-done | bytes 1048592 | tf_op jit(solution)/shard_map/psum | solution.py:191
  398.7 2.5 multiply_reduce_fusion.1
  406.7 3.9 convolution_bitcast_fusion
  414.1 3.4 fusion.11
  418.2 3.9 fusion.19
  422.2 42.8 %reduce-scatter.32.cloned.1.call-done = f32[128,1]{1,0:T(8,128)} async-done(((f32[1024,1]{1,0:T(8,128)}), f32[128,1]{1,0:T(8,128)}) %reduce-scatter.32.cloned.1.call-update) | async-done | bytes 528
  467.8 62.1 %reduce-scatter.30.cloned.1.call-done = f32[128,2]{1,0:T(8,128)} async-done(((f32[1024,2]{1,0:T(8,128)}), f32[128,2]{1,0:T(8,128)}) %reduce-scatter.30.cloned.1.call-update) | async-done | bytes 1040
  531.4 63.9 %reduce-scatter.28.cloned.1.call-done = f32[128,2]{1,0:T(8,128)} async-done(((f32[1024,2]{1,0:T(8,128)}), f32[128,2]{1,0:T(8,128)}) %reduce-scatter.28.cloned.1.call-update) | async-done | bytes 1040
  596.8 89.8 %reduce-scatter.26.cloned.1.call-done = f32[128,1024]{0,1:T(8,128)} async-done(((f32[1024,1024]{0,1:T(8,128)}), f32[128,1024]{0,1:T(8,128)}) %reduce-scatter.26.cloned.1.call-update) | async-done | bytes 524304 | tf_op jit(solution)/shard_map/reduce_scatter | solution.py:203
  688.7 65.8 %reduce-scatter.22.cloned.1.call-done = f32[128,256]{1,0:T(8,128)} async-done(((f32[1024,256]{1,0:T(8,128)}), f32[128,256]{1,0:T(8,128)}) %reduce-scatter.22.cloned.1.call-update) | async-done | bytes 131088 | tf_op jit(solution)/shard_map/reduce_scatter | solution.py:201
  754.5 78.0 %reduce-scatter.20.cloned.1.call-done = f32[128,3,256]{2,0,1:T(8,128)} async-done(((f32[1024,3,256]{2,0,1:T(8,128)}), f32[128,3,256]{2,0,1:T(8,128)}) %reduce-scatter.20.cloned.1.call-update) | async-done | bytes 393232 | tf_op jit(solution)/shard_map/reduce_scatter | solution.py:200
  832.4 91.5 %reduce-scatter.24.cloned.1.call-done = f32[128,1024]{1,0:T(8,128)} async-done(((f32[1024,1024]{1,0:T(8,128)}), f32[128,1024]{1,0:T(8,128)}) %reduce-scatter.24.cloned.1.call-update) | async-done | bytes 524304 | tf_op jit(solution)/shard_map/reduce_scatter | solution.py:202
  (156 shorter events, 49.8 us)
Async XLA Ops:
  7.2 78.8 %copy-start = (f32[2,128,1024]{2,1,0:T(8,128)S(1)}, f32[2,128,1024]{2,1,0:T(8,128)}, u32[]{:S(2)}) copy-start(f32[2,128,1024]{2,1,0:T(8,128)} %param.10) | copy-start | bytes 3145732
  7.2 47.3 %copy-start.28 = (s32[2,128]{1,0:T(2,128)S(1)}, s32[2,128]{1,0:T(2,128)}, u32[]{:S(2)}) copy-start(s32[2,128]{1,0:T(2,128)} %param.11) | copy-start | bytes 3076
  7.2 47.4 %copy-start.16 = (bf16[128,256]{1,0:T(8,128)(2,1)S(1)}, bf16[128,256]{1,0:T(8,128)(2,1)}, u32[]{:S(2)}) copy-start(bf16[128,256]{1,0:T(8,128)(2,1)} %param.15) | copy-start | bytes 196612
  7.2 79.1 %all-gather.4.cloned.1.call-start = ((), (), s32[]{:S(2)}) async-start(), calls=%async_computation.9 | async-start | bytes 1769472 | tf_op jit(solution)/shard_map/all_gather | solution.py:56
  7.9 131.7 %all-reduce.5.cloned.1.call-start = ((), (), s32[]{:S(2)}) async-start(), calls=%async_computation.10 | async-start | bytes 2097152 | tf_op jit(solution)/shard_map/psum | solution.py:110
  52.8 35.6 %copy-start.21 = (f32[256]{0:T(256)}, f32[256]{0:T(256)S(1)}, u32[]{:S(2)}) copy-start(f32[256]{0:T(256)S(1)} %get-tuple-element.54) | copy-start | bytes 3076
  54.3 34.1 %copy-start.23 = (f32[256]{0:T(256)}, f32[256]{0:T(256)S(1)}, u32[]{:S(2)}) copy-start(f32[256]{0:T(256)S(1)} %rsqrt_bitcast_fusion) | copy-start | bytes 3076
  54.4 137.0 %copy-start.19 = (f32[1,1024]{1,0:T(1,128)}, f32[1,1024]{1,0:T(1,128)S(1)}, u32[]{:S(2)}) copy-start(f32[1,1024]{1,0:T(1,128)S(1)} %get-tuple-element.52) | copy-start | bytes 12292
  86.0 16.5 %copy-start.3 = (bf16[1024,256]{1,0:T(8,128)(2,1)}, bf16[1024,256]{1,0:T(8,128)(2,1)S(1)}, u32[]{:S(2)}) copy-start(bf16[1024,256]{1,0:T(8,128)(2,1)S(1)} %all_gather.41) | copy-start | bytes 1572868
  102.5 23.8 %copy-start.14 = (bf16[2,128,4,64]{1,0,3,2:T(2,128)(2,1)}, bf16[2,128,4,64]{1,0,3,2:T(2,128)(2,1)S(1)}, u32[]{:S(2)}) copy-start(bf16[2,128,4,64]{1,0,3,2:T(2,128)(2,1)S(1)} %copy.48) | copy-start | bytes 393220
  104.3 87.0 %all-gather.6.cloned.1.call-start = ((), (), s32[]{:S(2)}) async-start(), calls=%async_computation.11 | async-start | bytes 2359296 | tf_op jit(solution)/shard_map/all_gather | solution.py:58
  105.1 135.9 %all-gather.8.cloned.1.call-start = ((), (), s32[]{:S(2)}) async-start(), calls=%async_computation.12 | async-start | bytes 2359296 | tf_op jit(solution)/shard_map/all_gather | solution.py:59
  105.7 176.8 %all-reduce.9.cloned.1.call-start = ((), (), s32[]{:S(2)}) async-start(), calls=%async_computation.14 | async-start | bytes 2097152 | tf_op jit(solution)/shard_map/psum | solution.py:142
  141.3 177.8 %copy-start.25 = (f32[256]{0:T(256)}, f32[256]{0:T(256)S(1)}, u32[]{:S(2)}) copy-start(f32[256]{0:T(256)S(1)} %add_rsqrt_fusion) | copy-start | bytes 3076
  247.5 71.6 %all-reduce.7.cloned.1.call-start = ((), (), s32[]{:S(2)}) async-start(), calls=%async_computation.13 | async-start | bytes 1048576 | tf_op jit(solution)/shard_map/psum | solution.py:123
  251.1 90.2 %reduce-scatter.18.cloned.1.call-start = ((), (), s32[]{:S(2)}) async-start(), calls=%async_computation.16 | async-start | bytes 786432 | tf_op jit(solution)/shard_map/reduce_scatter | solution.py:175
  326.3 31.8 %reduce-scatter.16.cloned.1.call-start = ((), (), s32[]{:S(2)}) async-start(), calls=%async_computation.15 | async-start | bytes 786432 | tf_op jit(solution)/shard_map/reduce_scatter | solution.py:174
  330.7 68.0 %all-reduce.11.cloned.1.call-start = ((), (), s32[]{:S(2)}) async-start(), calls=%async_computation.17 | async-start | bytes 2097152 | tf_op jit(solution)/shard_map/psum | solution.py:191
  362.3 102.8 %reduce-scatter.32.cloned.1.call-start = ((), (), s32[]{:S(2)}) async-start(), calls=%async_computation.24 | async-start | bytes 589824
  362.3 41.3 %copy-start.17 = (f32[1024]{0:T(1024)S(1)}, f32[1024]{0:T(1024)}, u32[]{:S(2)}) copy-start(f32[1024]{0:T(1024)} %get-tuple-element.38) | copy-start | bytes 12292
  363.4 43.3 %copy-start.8 = (f32[256,1024]{1,0:T(8,128)S(1)}, f32[256,1024]{1,0:T(8,128)}, u32[]{:S(2)}) copy-start(f32[256,1024]{1,0:T(8,128)} %convolution_add_fusion) | copy-start | bytes 3145732
  363.4 166.6 %reduce-scatter.30.cloned.1.call-start = ((), (), s32[]{:S(2)}) async-start(), calls=%async_computation.23 | async-start | bytes 589824
  403.5 191.8 %reduce-scatter.28.cloned.1.call-start = ((), (), s32[]{:S(2)}) async-start(), calls=%async_computation.22 | async-start | bytes 589824
  406.6 280.0 %reduce-scatter.26.cloned.1.call-start = ((), (), s32[]{:S(2)}) async-start(), calls=%async_computation.21 | async-start | bytes 4718592 | tf_op jit(solution)/shard_map/reduce_scatter | solution.py:203
  410.6 343.9 %reduce-scatter.22.cloned.1.call-start = ((), (), s32[]{:S(2)}) async-start(), calls=%async_computation.19 | async-start | bytes 1179648 | tf_op jit(solution)/shard_map/reduce_scatter | solution.py:201
  414.1 418.3 %reduce-scatter.20.cloned.1.call-start = ((), (), s32[]{:S(2)}) async-start(), calls=%async_computation.18 | async-start | bytes 3538944 | tf_op jit(solution)/shard_map/reduce_scatter | solution.py:200
  417.6 506.4 %reduce-scatter.24.cloned.1.call-start = ((), (), s32[]{:S(2)}) async-start(), calls=%async_computation.20 | async-start | bytes 4718592 | tf_op jit(solution)/shard_map/reduce_scatter | solution.py:202
  422.1 44.3 %copy-start.30 = (f32[256]{0:T(256)S(1)}, f32[256]{0:T(256)}, u32[]{:S(2)}) copy-start(f32[256]{0:T(256)} %get-tuple-element.37) | copy-start | bytes 3076
  422.1 44.3 %copy-start.29 = (f32[256]{0:T(256)S(1)}, f32[256]{0:T(256)}, u32[]{:S(2)}) copy-start(f32[256]{0:T(256)} %get-tuple-element.41) | copy-start | bytes 3076
  422.1 44.3 %copy-start.7 = (f32[256,1024]{1,0:T(8,128)S(1)}, f32[256,1024]{1,0:T(8,128)}, u32[]{:S(2)}) copy-start(f32[256,1024]{1,0:T(8,128)} %all-reduce.11.cloned.1.call-done) | copy-start | bytes 3145732
  422.1 44.3 %copy-start.22 = (f32[256]{0:T(256)S(1)}, f32[256]{0:T(256)}, u32[]{:S(2)}) copy-start(f32[256]{0:T(256)} %copy-done.21) | copy-start | bytes 3076
  422.1 44.4 %copy-start.24 = (f32[256]{0:T(256)S(1)}, f32[256]{0:T(256)}, u32[]{:S(2)}) copy-start(f32[256]{0:T(256)} %copy-done.23) | copy-start | bytes 3076
  (16 other events, 37.4 us)
Sparse Core Ops, SparseCore 0:
  10.2 47.6 all-gather.3
  104.5 35.1 all-reduce.4
  141.8 49.5 all-gather.5
  193.3 47.6 all-gather.7
  247.6 34.8 all-reduce.8
  285.2 33.8 all-reduce.6
  326.5 14.7 reduce-scatter.17
  343.5 14.6 reduce-scatter.15
  362.4 36.2 all-reduce.10
  401.9 63.0 reduce-scatter.31
  468.4 61.5 reduce-scatter.29
  533.7 61.5 reduce-scatter.27
  599.0 87.6 reduce-scatter.25
  690.5 63.9 reduce-scatter.21
  758.5 73.8 reduce-scatter.19
  836.5 87.4 reduce-scatter.23
where the time goes:
time: 932 us; the launch traced here: 930 us
  waiting for transfers between devices  731 us (78%)
  blocking collectives  105 us (11%)
  matrix products  38.5 us (4%)
  other arithmetic  21.5 us (2%)
  local copies, waits for them, and re-layouts  19.6 us (2%)
  between operations  14.5 us (2%)
    unnamed x19, waiting for transfers between devices  171 us
    reduce_scatter x1, waiting for transfers between devices, shards(): lax.psum_scatter(expand_grad, ('shard', 'ctx'), scatter_dimension=0, tile...  91.5 us
    reduce_scatter x1, waiting for transfers between devices, shards(): lax.psum_scatter(reduce_grad, ('shard', 'ctx'), scatter_dimension=0, tile...  89.8 us
    reduce_scatter x1, waiting for transfers between devices, shards(): lax.psum_scatter(attend_grad, ('shard', 'ctx'), scatter_dimension=0, tile...  78 us
    reduce_scatter x1, waiting for transfers between devices, shards(): lax.psum_scatter(merge_grad, ('shard', 'ctx'), scatter_dimension=0, tiled...  65.8 us
    all_gather x1, waiting for transfers between devices, shards(): lax.all_gather(expand_weight, ('shard', 'ctx'), axis=0, tiled=True)  50 us
    all_gather x1, waiting for transfers between devices, shards(): lax.all_gather(reduce_weight, ('shard', 'ctx'), axis=0, tiled=True)  46.3 us
    psum x1, waiting for transfers between devices, shards(): early_grad = lax.psum(early_part, 'tp')  35.1 us
  transfers between devices with their start and end apart: 16, of which 15 were waited for; matrix products, arithmetic and copies ran while one was open for 6% of the time, Pallas kernels for 0%

commit v1 on v0

--- a/solution.py
+++ b/solution.py
@@ -139,7 +139,7 @@
         "rd,rf->df", hidden_later, pre_half, preferred_element_type=jnp.float32
     )
     later_part = jnp.einsum("rf,df->rd", pre_half, expand_back, preferred_element_type=jnp.float32)
-    later_grad = lax.psum(later_part, "tp")
+    later_grad = jnp.sum(lax.all_gather(later_part, "tp"), axis=0)
     residual_grad = output_grad + norm_backward(
         later_grad, normed_later, inverse_later, gains_back[1]
     )

time: 932 us -> 930 us (level)
    psum x1 -> x0, waiting for transfers between devices: 31.3 us -> none  [shards(): later_grad = lax.psum(later_part, 'tp')]
    all_gather x0 -> x1, waiting for transfers between devices: none -> 29.5 us  [shards(): later_grad = jnp.sum(lax.all_gather(later_part, 'tp'), axis=0)]
where the time goes in v1:
time: 930 us; the launch traced here: 928 us
  waiting for transfers between devices  723 us (78%)
  blocking collectives  105 us (11%)
  matrix products  37.5 us (4%)
  other arithmetic  28.2 us (3%)
  local copies, waits for them, and re-layouts  19.9 us (2%)
  between operations  14.5 us (2%)
    unnamed x19, waiting for transfers between devices  172 us
    reduce_scatter x1, waiting for transfers between devices, shards(): lax.psum_scatter(expand_grad, ('shard', 'ctx'), scatter_dimension=0, tile...  91.4 us
    reduce_scatter x1, waiting for transfers between devices, shards(): lax.psum_scatter(reduce_grad, ('shard', 'ctx'), scatter_dimension=0, tile...  89.8 us
    reduce_scatter x1, waiting for transfers between devices, shards(): lax.psum_scatter(attend_grad, ('shard', 'ctx'), scatter_dimension=0, tile...  78.4 us
    reduce_scatter x1, waiting for transfers between devices, shards(): lax.psum_scatter(merge_grad, ('shard', 'ctx'), scatter_dimension=0, tiled...  65.6 us
    all_gather x1, waiting for transfers between devices, shards(): lax.all_gather(expand_weight, ('shard', 'ctx'), axis=0, tiled=True)  50 us
    all_gather x1, waiting for transfers between devices, shards(): lax.all_gather(reduce_weight, ('shard', 'ctx'), axis=0, tiled=True)  46.3 us
    psum x1, waiting for transfers between devices, shards(): early_grad = lax.psum(early_part, 'tp')  32 us
  transfers between devices with their start and end apart: 16, of which 15 were waited for; matrix products, arithmetic and copies ran while one was open for 6% of the time, Pallas kernels for 0%

profile of v1, /device:TPU:0, one launch (start us, length us, event | category | flops | bytes accessed | tf_op | source)
XLA Modules:
  0.0 928.4 jit_solution(8659205784292904864)
XLA Ops:
  9.4 5.5 all_gather.45
  14.8 21.4 %all_gather.41 = bf16[2,1024]{1,0:T(2,128)(2,1)S(1)} all-gather(bf16[2,128]{1,0:T(2,128)(2,1)} %param.12), channel_id=1, replica_groups=mesh['shard'=4,'ctx'=2,'tp'=4] {'shard','ctx'}, dimensions={1}, use_global_device_ids=true | all-gather | bytes 4608 | tf_op jit(solution)/shard_map/all_gather | solution.py:61
  36.3 16.5 %all_gather.42 = bf16[2,1024]{1,0:T(2,128)(2,1)S(1)} all-gather(bf16[2,128]{1,0:T(2,128)(2,1)} %param.13), channel_id=1, replica_groups=mesh['shard'=4,'ctx'=2,'tp'=4] {'shard','ctx'}, dimensions={1}, use_global_device_ids=true | all-gather | bytes 4608 | tf_op jit(solution)/shard_map/all_gather | solution.py:62
  54.6 31.4 %all_gather.47 = bf16[1024,256]{1,0:T(8,128)(2,1)S(1)} all-gather(bf16[128,256]{1,0:T(8,128)(2,1)S(1)} %copy-done.17), channel_id=1, replica_groups=mesh['shard'=4,'ctx'=2,'tp'=4] {'shard','ctx'}, dimensions={0}, use_global_device_ids=true | all-gather | bytes 589824 | tf_op jit(solution)/shard_map/all_gather | solution.py:57
  88.5 5.6 all_gather.44
  95.0 5.6 all_gather.46
  105.7 18.4 %all_gather.49 = bf16[1,1024]{1,0:T(2,128)(2,1)S(1)} all-gather(bf16[1,128]{1,0:T(2,128)(2,1)S(1)} %copy-done.31), channel_id=1, replica_groups=mesh['shard'=4,'ctx'=2,'tp'=4] {'shard','ctx'}, dimensions={1}, use_global_device_ids=true | all-gather | bytes 2304 | tf_op jit(solution)/shard_map/all_gather | solution.py:60
  126.2 13.4 %all-reduce.4.cloned.1.call-done = f32[256,1024]{1,0:T(8,128)} async-done(((f32[256,1024]{1,0:T(8,128)}), f32[256,1024]{1,0:T(8,128)}) %all-reduce.4.cloned.1.call-update) | async-done | bytes 1048592 | tf_op jit(solution)/shard_map/psum | solution.py:110
  141.3 50.0 %all-gather.8.cloned.1.call-done = bf16[1024,1024]{1,0:T(8,128)(2,1)} async-done(((bf16[128,1024]{1,0:T(8,128)(2,1)}), bf16[1024,1024]{1,0:T(8,128)(2,1)}) %all-gather.8.cloned.1.call-update) | async-done | bytes 2097168 | tf_op jit(solution)/shard_map/all_gather | solution.py:58
  191.4 3.3 convolution_add_fusion
  194.7 46.3 %all-gather.10.cloned.1.call-done = bf16[1024,1024]{1,0:T(8,128)(2,1)} async-done(((bf16[128,1024]{1,0:T(8,128)(2,1)}), bf16[1024,1024]{1,0:T(8,128)(2,1)}) %all-gather.10.cloned.1.call-update) | async-done | bytes 2097168 | tf_op jit(solution)/shard_map/all_gather | solution.py:59
  241.0 3.9 fusion.40
  247.6 3.5 convolution_convert_fusion
  251.2 29.5 %all-gather.12.cloned.1.call-done = f32[1024,1024]{1,0:T(8,128)} async-done(((f32[256,1024]{1,0:T(8,128)}), f32[1024,1024]{1,0:T(8,128)}) %all-gather.12.cloned.1.call-update) | async-done | bytes 4194320 | tf_op jit(solution)/shard_map/all_gather | solution.py:142
  280.6 3.7 reduce_sum.140
  286.6 30.2 %all-reduce.6.cloned.1.call-done = bf16[256,1024]{1,0:T(8,128)(2,1)} async-done(((bf16[256,1024]{1,0:T(8,128)(2,1)}), bf16[256,1024]{1,0:T(8,128)(2,1)}) %all-reduce.6.cloned.1.call-update) | async-done | bytes 524304 | tf_op jit(solution)/shard_map/psum | solution.py:123
  316.9 3.0 bitcast_add_fusion
  330.3 8.6 reduce-scatter.18.cloned.1.call-done
  340.1 15.8 %reduce-scatter.16.cloned.1.call-done = f32[2,128,256]{1,2,0:T(8,128)} async-done(((f32[2,256,256]{1,2,0:T(8,128)}), f32[2,128,256]{1,2,0:T(8,128)}) %reduce-scatter.16.cloned.1.call-update) | async-done | bytes 262160 | tf_op jit(solution)/shard_map/reduce_scatter | solution.py:174
  357.0 3.0 convolution_bitcast_fusion.1
  361.4 3.1 reduce_sum.148
  364.4 32.0 %all-reduce.8.cloned.1.call-done = f32[256,1024]{1,0:T(8,128)} async-done(((f32[256,1024]{1,0:T(8,128)}), f32[256,1024]{1,0:T(8,128)}) %all-reduce.8.cloned.1.call-update) | async-done | bytes 1048592 | tf_op jit(solution)/shard_map/psum | solution.py:191
  396.5 2.5 multiply_reduce_fusion.1
  404.4 3.9 convolution_bitcast_fusion
  411.9 3.9 fusion.19
  419.2 43.6 %reduce-scatter.32.cloned.1.call-done = f32[128,1]{1,0:T(8,128)} async-done(((f32[1024,1]{1,0:T(8,128)}), f32[128,1]{1,0:T(8,128)}) %reduce-scatter.32.cloned.1.call-update) | async-done | bytes 528
  465.6 62.2 %reduce-scatter.30.cloned.1.call-done = f32[128,2]{1,0:T(8,128)} async-done(((f32[1024,2]{1,0:T(8,128)}), f32[128,2]{1,0:T(8,128)}) %reduce-scatter.30.cloned.1.call-update) | async-done | bytes 1040
  529.2 63.9 %reduce-scatter.28.cloned.1.call-done = f32[128,2]{1,0:T(8,128)} async-done(((f32[1024,2]{1,0:T(8,128)}), f32[128,2]{1,0:T(8,128)}) %reduce-scatter.28.cloned.1.call-update) | async-done | bytes 1040
  594.6 89.8 %reduce-scatter.26.cloned.1.call-done = f32[128,1024]{0,1:T(8,128)} async-done(((f32[1024,1024]{0,1:T(8,128)}), f32[128,1024]{0,1:T(8,128)}) %reduce-scatter.26.cloned.1.call-update) | async-done | bytes 524304 | tf_op jit(solution)/shard_map/reduce_scatter | solution.py:203
  686.5 65.6 %reduce-scatter.22.cloned.1.call-done = f32[128,256]{1,0:T(8,128)} async-done(((f32[1024,256]{1,0:T(8,128)}), f32[128,256]{1,0:T(8,128)}) %reduce-scatter.22.cloned.1.call-update) | async-done | bytes 131088 | tf_op jit(solution)/shard_map/reduce_scatter | solution.py:201
  752.1 91.4 %reduce-scatter.24.cloned.1.call-done = f32[128,1024]{1,0:T(8,128)} async-done(((f32[1024,1024]{1,0:T(8,128)}), f32[128,1024]{1,0:T(8,128)}) %reduce-scatter.24.cloned.1.call-update) | async-done | bytes 524304 | tf_op jit(solution)/shard_map/reduce_scatter | solution.py:202
  843.6 78.4 %reduce-scatter.20.cloned.1.call-done = f32[128,3,256]{2,0,1:T(8,128)} async-done(((f32[1024,3,256]{2,0,1:T(8,128)}), f32[128,3,256]{2,0,1:T(8,128)}) %reduce-scatter.20.cloned.1.call-update) | async-done | bytes 393232 | tf_op jit(solution)/shard_map/reduce_scatter | solution.py:200
  (158 shorter events, 54.8 us)
Async XLA Ops:
  7.2 78.8 %copy-start = (f32[2,128,1024]{2,1,0:T(8,128)S(1)}, f32[2,128,1024]{2,1,0:T(8,128)}, u32[]{:S(2)}) copy-start(f32[2,128,1024]{2,1,0:T(8,128)} %param.10) | copy-start | bytes 3145732
  7.2 47.3 %copy-start.28 = (s32[2,128]{1,0:T(2,128)S(1)}, s32[2,128]{1,0:T(2,128)}, u32[]{:S(2)}) copy-start(s32[2,128]{1,0:T(2,128)} %param.11) | copy-start | bytes 3076
  7.2 47.4 %copy-start.17 = (bf16[128,256]{1,0:T(8,128)(2,1)S(1)}, bf16[128,256]{1,0:T(8,128)(2,1)}, u32[]{:S(2)}) copy-start(bf16[128,256]{1,0:T(8,128)(2,1)} %param.15) | copy-start | bytes 196612
  7.2 79.1 %all-gather.6.cloned.1.call-start = ((), (), s32[]{:S(2)}) async-start(), calls=%async_computation.9 | async-start | bytes 1769472 | tf_op jit(solution)/shard_map/all_gather | solution.py:56
  7.9 131.7 %all-reduce.4.cloned.1.call-start = ((), (), s32[]{:S(2)}) async-start(), calls=%async_computation.10 | async-start | bytes 2097152 | tf_op jit(solution)/shard_map/psum | solution.py:110
  52.8 35.6 %copy-start.22 = (f32[256]{0:T(256)}, f32[256]{0:T(256)S(1)}, u32[]{:S(2)}) copy-start(f32[256]{0:T(256)S(1)} %get-tuple-element.53) | copy-start | bytes 3076
  54.3 34.1 %copy-start.24 = (f32[256]{0:T(256)}, f32[256]{0:T(256)S(1)}, u32[]{:S(2)}) copy-start(f32[256]{0:T(256)S(1)} %rsqrt_bitcast_fusion) | copy-start | bytes 3076
  54.4 137.0 %copy-start.20 = (f32[1,1024]{1,0:T(1,128)}, f32[1,1024]{1,0:T(1,128)S(1)}, u32[]{:S(2)}) copy-start(f32[1,1024]{1,0:T(1,128)S(1)} %get-tuple-element.51) | copy-start | bytes 12292
  86.0 16.5 %copy-start.3 = (bf16[1024,256]{1,0:T(8,128)(2,1)}, bf16[1024,256]{1,0:T(8,128)(2,1)S(1)}, u32[]{:S(2)}) copy-start(bf16[1024,256]{1,0:T(8,128)(2,1)S(1)} %all_gather.47) | copy-start | bytes 1572868
  102.5 23.7 %copy-start.15 = (bf16[2,128,4,64]{1,0,3,2:T(2,128)(2,1)}, bf16[2,128,4,64]{1,0,3,2:T(2,128)(2,1)S(1)}, u32[]{:S(2)}) copy-start(bf16[2,128,4,64]{1,0,3,2:T(2,128)(2,1)S(1)} %copy.48) | copy-start | bytes 393220
  104.3 87.0 %all-gather.8.cloned.1.call-start = ((), (), s32[]{:S(2)}) async-start(), calls=%async_computation.11 | async-start | bytes 2359296 | tf_op jit(solution)/shard_map/all_gather | solution.py:58
  105.1 135.9 %all-gather.10.cloned.1.call-start = ((), (), s32[]{:S(2)}) async-start(), calls=%async_computation.12 | async-start | bytes 2359296 | tf_op jit(solution)/shard_map/all_gather | solution.py:59
  105.6 175.0 %all-gather.12.cloned.1.call-start = ((), (), s32[]{:S(2)}) async-start(), calls=%async_computation.21 | async-start | bytes 5242880 | tf_op jit(solution)/shard_map/all_gather | solution.py:142
  141.3 175.6 %copy-start.26 = (f32[256]{0:T(256)}, f32[256]{0:T(256)S(1)}, u32[]{:S(2)}) copy-start(f32[256]{0:T(256)S(1)} %add_rsqrt_fusion) | copy-start | bytes 3076
  247.5 69.3 %all-reduce.6.cloned.1.call-start = ((), (), s32[]{:S(2)}) async-start(), calls=%async_computation.13 | async-start | bytes 1048576 | tf_op jit(solution)/shard_map/psum | solution.py:123
  251.1 87.9 %reduce-scatter.18.cloned.1.call-start = ((), (), s32[]{:S(2)}) async-start(), calls=%async_computation.15 | async-start | bytes 786432 | tf_op jit(solution)/shard_map/reduce_scatter | solution.py:175
  324.1 31.8 %reduce-scatter.16.cloned.1.call-start = ((), (), s32[]{:S(2)}) async-start(), calls=%async_computation.14 | async-start | bytes 786432 | tf_op jit(solution)/shard_map/reduce_scatter | solution.py:174
  328.5 67.9 %all-reduce.8.cloned.1.call-start = ((), (), s32[]{:S(2)}) async-start(), calls=%async_computation.16 | async-start | bytes 2097152 | tf_op jit(solution)/shard_map/psum | solution.py:191
  360.0 102.7 %reduce-scatter.32.cloned.1.call-start = ((), (), s32[]{:S(2)}) async-start(), calls=%async_computation.24 | async-start | bytes 589824
  361.1 166.6 %reduce-scatter.30.cloned.1.call-start = ((), (), s32[]{:S(2)}) async-start(), calls=%async_computation.23 | async-start | bytes 589824
  364.4 36.9 %copy-start.18 = (f32[1024]{0:T(1024)S(1)}, f32[1024]{0:T(1024)}, u32[]{:S(2)}) copy-start(f32[1024]{0:T(1024)} %get-tuple-element.38) | copy-start | bytes 12292
  364.4 40.0 %copy-start.9 = (f32[256,1024]{1,0:T(8,128)S(1)}, f32[256,1024]{1,0:T(8,128)}, u32[]{:S(2)}) copy-start(f32[256,1024]{1,0:T(8,128)} %convolution_add_fusion) | copy-start | bytes 3145732
  401.3 191.9 %reduce-scatter.28.cloned.1.call-start = ((), (), s32[]{:S(2)}) async-start(), calls=%async_computation.22 | async-start | bytes 589824
  404.4 280.1 %reduce-scatter.26.cloned.1.call-start = ((), (), s32[]{:S(2)}) async-start(), calls=%async_computation.20 | async-start | bytes 4718592 | tf_op jit(solution)/shard_map/reduce_scatter | solution.py:203
  408.3 343.8 %reduce-scatter.22.cloned.1.call-start = ((), (), s32[]{:S(2)}) async-start(), calls=%async_computation.18 | async-start | bytes 1179648 | tf_op jit(solution)/shard_map/reduce_scatter | solution.py:201
  411.8 431.7 %reduce-scatter.24.cloned.1.call-start = ((), (), s32[]{:S(2)}) async-start(), calls=%async_computation.19 | async-start | bytes 4718592 | tf_op jit(solution)/shard_map/reduce_scatter | solution.py:202
  415.8 506.1 %reduce-scatter.20.cloned.1.call-start = ((), (), s32[]{:S(2)}) async-start(), calls=%async_computation.17 | async-start | bytes 3538944 | tf_op jit(solution)/shard_map/reduce_scatter | solution.py:200
  419.2 45.0 %copy-start.30 = (f32[256]{0:T(256)S(1)}, f32[256]{0:T(256)}, u32[]{:S(2)}) copy-start(f32[256]{0:T(256)} %get-tuple-element.37) | copy-start | bytes 3076
  419.2 45.0 %copy-start.29 = (f32[256]{0:T(256)S(1)}, f32[256]{0:T(256)}, u32[]{:S(2)}) copy-start(f32[256]{0:T(256)} %get-tuple-element.41) | copy-start | bytes 3076
  419.2 45.0 %copy-start.8 = (f32[256,1024]{1,0:T(8,128)S(1)}, f32[256,1024]{1,0:T(8,128)}, u32[]{:S(2)}) copy-start(f32[256,1024]{1,0:T(8,128)} %all-reduce.8.cloned.1.call-done) | copy-start | bytes 3145732
  419.2 45.1 %copy-start.23 = (f32[256]{0:T(256)S(1)}, f32[256]{0:T(256)}, u32[]{:S(2)}) copy-start(f32[256]{0:T(256)} %copy-done.22) | copy-start | bytes 3076
  419.2 45.1 %copy-start.25 = (f32[256]{0:T(256)S(1)}, f32[256]{0:T(256)}, u32[]{:S(2)}) copy-start(f32[256]{0:T(256)} %copy-done.24) | copy-start | bytes 3076
  (16 other events, 40.7 us)
Sparse Core Ops, SparseCore 0:
  10.2 47.6 all-gather.5
  104.5 35.1 all-reduce.3
  141.8 49.5 all-gather.7
  193.3 47.6 all-gather.9
  247.6 32.9 all-gather.11
  283.4 33.3 all-reduce.5
  324.2 14.7 reduce-scatter.17
  341.2 14.6 reduce-scatter.15
  360.1 36.2 all-reduce.7
  399.7 63.0 reduce-scatter.31
  466.1 61.5 reduce-scatter.29
  531.5 61.5 reduce-scatter.27
  596.8 87.6 reduce-scatter.25
  688.3 63.7 reduce-scatter.21
  756.2 87.3 reduce-scatter.23
  847.6 74.2 reduce-scatter.19
